TPU v7x, 32 devices: a whole 2x2x4 slice. The times are simulated.
32 devices in a mesh: bin: 4 (over x, core), fsdp: 8 (over z, y).
Axes of the slice: x: 2, y: 2, z: 4, core: 2. Of those that a mesh axis runs over, the one named last changes fastest.
Arguments:
- latents: bfloat16 [4, 16, 256, 1152], P('bin', 'fsdp'), may hold values from -6 to 6
- cond: float32 [4, 1152], P('bin'), may hold values from -6 to 6
- live: int32 [4, 8], P('bin', 'fsdp'), may hold values from 1 to 2, 12 in all within a row
- w_ada: bfloat16 [1152, 6912], P(None, 'fsdp'), may hold values from -0.375 to 0.375
- b_ada: bfloat16 [6912], P('fsdp'), may hold values from -3 to 3
- w_qkv: bfloat16 [1152, 3456], P('fsdp'), may hold values from -0.1875 to 0.1875
- b_qv: bfloat16 [2304], P('fsdp'), may hold values from -3 to 3
- w_proj: bfloat16 [1152, 1152], P('fsdp'), may hold values from -0.5 to 0.5
- b_proj: bfloat16 [1152], P('fsdp'), may hold values from -3 to 3
- w_fc1: bfloat16 [1152, 4608], P('fsdp'), may hold values from -0.1875 to 0.1875
- b_fc1: bfloat16 [4608], P('fsdp'), may hold values from -3 to 3
- w_fc2: bfloat16 [4608, 1152], P('fsdp'), may hold values from -0.09375 to 0.09375
- b_fc2: bfloat16 [1152], P('fsdp'), may hold values from -3 to 3
- cotangent: bfloat16 [4, 16, 256, 1152], P('bin', 'fsdp'), may hold values from -6 to 6
Outputs:
- block_out: bfloat16 [4, 16, 256, 1152], P('bin', 'fsdp')
- latents_grad: float32 [4, 16, 256, 1152], P('bin', 'fsdp')
- cond_grad: float32 [4, 1152], P('bin')
- w_ada_grad: float32 [1152, 6912], P(None, 'fsdp')
- b_ada_grad: float32 [6912], P('fsdp')
- w_qkv_grad: float32 [1152, 3456], P('fsdp')
- b_qv_grad: float32 [2304], P('fsdp')
- w_proj_grad: float32 [1152, 1152], P('fsdp')
- b_proj_grad: float32 [1152], P('fsdp')
- w_fc1_grad: float32 [1152, 4608], P('fsdp')
- b_fc1_grad: float32 [4608], P('fsdp')
- w_fc2_grad: float32 [4608, 1152], P('fsdp')
- b_fc2_grad: float32 [1152], P('fsdp')
Inputs may be any that keep to these rules, and one draw needn't show every extreme that they name: The counts of one bin's devices sum to 12; every bin has a device with 2 live images; a device's live images are its first slots.
All inputs are finite; a program needn't handle non-finite values.
Results may differ from a plain program's by a relative error of at most 0.015.
The roundings to bfloat16 on the way count: a program that leaves them out, or rounds other values in their place, can miss the bound.
Values may be sent and summed in bfloat16 or wider, within the bound.
A program may use at most 256 MiB of HBM per device.

v0:
```python
import jax
import jax.numpy as jnp
from jax import lax
from jax.sharding import PartitionSpec as P

HEAD_DIM = 72


def layer_norm(field):
    center = field - jnp.mean(field, axis=-1, keepdims=True)
    return center * lax.rsqrt(jnp.mean(center * center, axis=-1, keepdims=True) + 1e-06)


def gelu_tanh(field):
    return (
        0.5
        * field
        * (1.0 + jnp.tanh(0.7978845608028654 * (field + 0.044715 * field * field * field)))
    )


def modulate(field, shift_vec, scale_vec):
    return layer_norm(field) * (1.0 + scale_vec) + shift_vec


def pair_scores(query_block, key_block):
    return jnp.einsum(
        "gqhd,gkhd->ghqk", query_block, key_block, preferred_element_type=jnp.float32
    ) * HEAD_DIM ** (-0.5)


def attend_pair(group_item):
    query_block, key_block, value_block = group_item
    scores = pair_scores(query_block, key_block)
    highest = jnp.max(scores, axis=-1, keepdims=True)
    exp_scores = jnp.exp(scores - highest)
    totals = jnp.sum(exp_scores, axis=-1, keepdims=True)
    attn_probs = (exp_scores / totals).astype(jnp.bfloat16)
    attended = jnp.einsum(
        "ghqk,gkhd->gqhd", attn_probs, value_block, preferred_element_type=jnp.float32
    )
    return (attended, (highest + jnp.log(totals))[..., 0])


def attend_back(group_item):
    query_block, key_block, value_block, log_total, grad_att = group_item
    scores = pair_scores(query_block, key_block)
    attn_probs = jnp.exp(scores - log_total[..., None])
    grad_probs = jnp.einsum(
        "gqhd,gkhd->ghqk", grad_att, value_block, preferred_element_type=jnp.float32
    )
    row_terms = jnp.sum(attn_probs * grad_probs, axis=-1, keepdims=True)
    grad_scores = (attn_probs * (grad_probs - row_terms)).astype(jnp.bfloat16)
    grad_query = jnp.einsum(
        "ghqk,gkhd->gqhd", grad_scores, key_block, preferred_element_type=jnp.float32
    ) * HEAD_DIM ** (-0.5)
    grad_key = jnp.einsum(
        "ghqk,gqhd->gkhd", grad_scores, query_block, preferred_element_type=jnp.float32
    ) * HEAD_DIM ** (-0.5)
    grad_value = jnp.einsum(
        "ghqk,gqhd->gkhd",
        attn_probs.astype(jnp.bfloat16),
        grad_att,
        preferred_element_type=jnp.float32,
    )
    return jnp.stack([grad_query, grad_key, grad_value], axis=2)


def run_block(flat_rows, modulation, weights, images, length):
    full_qkv, full_proj, full_fc1, full_fc2, bias_qv, bias_proj, bias_fc1, bias_fc2 = weights
    width = flat_rows.shape[1]
    heads = width // HEAD_DIM
    pieces = jnp.split(modulation, 6)
    h_first = modulate(flat_rows, pieces[0], pieces[1]).astype(jnp.bfloat16)
    qkv_bias = jnp.concatenate(
        [bias_qv[:width], jnp.zeros((width,), jnp.bfloat16), bias_qv[width:]]
    ).astype(jnp.float32)
    qkv_rows = (jnp.dot(h_first, full_qkv, preferred_element_type=jnp.float32) + qkv_bias).astype(
        jnp.bfloat16
    )
    split_rows = qkv_rows.reshape(images // 2, 2, length, 3, heads, HEAD_DIM)
    attended, log_total = lax.map(
        attend_pair, (split_rows[:, :, :, 0], split_rows[:, :, :, 1], split_rows[:, :, :, 2])
    )
    attended = attended.reshape(images * length, width).astype(jnp.bfloat16)
    branch = jnp.dot(attended, full_proj, preferred_element_type=jnp.float32) + bias_proj.astype(
        jnp.float32
    )
    middle = flat_rows + pieces[2] * branch
    h_second = modulate(middle, pieces[3], pieces[4]).astype(jnp.bfloat16)
    pre_act = jnp.dot(h_second, full_fc1, preferred_element_type=jnp.float32) + bias_fc1.astype(
        jnp.float32
    )
    hidden = gelu_tanh(pre_act).astype(jnp.bfloat16)
    mlp_out = jnp.dot(hidden, full_fc2, preferred_element_type=jnp.float32) + bias_fc2.astype(
        jnp.float32
    )
    result = middle + pieces[5] * mlp_out
    return (
        h_first,
        split_rows,
        log_total,
        attended,
        branch,
        middle,
        h_second,
        pre_act,
        hidden,
        mlp_out,
        result,
    )


def on_device(
    latents,
    cond,
    live,
    w_ada,
    b_ada,
    w_qkv,
    b_qv,
    w_proj,
    b_proj,
    w_fc1,
    b_fc1,
    w_fc2,
    b_fc2,
    cotangent,
):
    images = latents.shape[1]
    length = latents.shape[2]
    width = latents.shape[3]
    heads = width // HEAD_DIM
    scaled = jax.nn.silu(cond[0]).astype(jnp.bfloat16)
    mod_part = jnp.dot(scaled, w_ada, preferred_element_type=jnp.float32) + b_ada.astype(
        jnp.float32
    )
    modulation = lax.all_gather(mod_part, "fsdp", axis=0, tiled=True)
    gathered = (
        lax.all_gather(w_qkv, "fsdp", axis=0, tiled=True),
        lax.all_gather(w_proj, "fsdp", axis=0, tiled=True),
        lax.all_gather(w_fc1, "fsdp", axis=0, tiled=True),
        lax.all_gather(w_fc2, "fsdp", axis=0, tiled=True),
        lax.all_gather(b_qv, "fsdp", axis=0, tiled=True),
        lax.all_gather(b_proj, "fsdp", axis=0, tiled=True),
        lax.all_gather(b_fc1, "fsdp", axis=0, tiled=True),
        lax.all_gather(b_fc2, "fsdp", axis=0, tiled=True),
    )
    flat_rows = latents[0].reshape(images * length, width).astype(jnp.float32)
    live_mask = (lax.iota(jnp.int32, images) < live[0, 0]).astype(jnp.float32)
    row_mask = jnp.repeat(live_mask, length)[:, None]
    forward_run = run_block(flat_rows, modulation, gathered, images, length)
    block_out = (forward_run[10] * row_mask).astype(jnp.bfloat16).reshape(latents.shape)
    weights = (
        lax.all_gather(w_qkv, "fsdp", axis=0, tiled=True),
        lax.all_gather(w_proj, "fsdp", axis=0, tiled=True),
        lax.all_gather(w_fc1, "fsdp", axis=0, tiled=True),
        lax.all_gather(w_fc2, "fsdp", axis=0, tiled=True),
        lax.all_gather(b_qv, "fsdp", axis=0, tiled=True),
        lax.all_gather(b_proj, "fsdp", axis=0, tiled=True),
        lax.all_gather(b_fc1, "fsdp", axis=0, tiled=True),
        lax.all_gather(b_fc2, "fsdp", axis=0, tiled=True),
    )
    full_qkv, full_proj, full_fc1, full_fc2 = (weights[0], weights[1], weights[2], weights[3])
    saved = run_block(flat_rows, modulation, weights, images, length)
    (
        h_first,
        split_rows,
        log_total,
        attended,
        branch,
        middle,
        h_second,
        pre_act,
        hidden,
        mlp_out,
        result,
    ) = saved
    pieces = jnp.split(modulation, 6)
    grad_res = cotangent[0].reshape(images * length, width).astype(jnp.float32) * row_mask
    grad_out = (pieces[5] * grad_res).astype(jnp.bfloat16)
    grad_gate_two = jnp.sum(grad_res * mlp_out, axis=0)
    grad_fc2 = jnp.einsum("rf,rd->fd", hidden, grad_out, preferred_element_type=jnp.float32)
    grad_bfc2 = jnp.sum(grad_out.astype(jnp.float32), axis=0)
    grad_hidden = jnp.einsum("rd,fd->rf", grad_out, full_fc2, preferred_element_type=jnp.float32)
    gelu_pull = jax.vjp(gelu_tanh, pre_act)[1]
    grad_pre = gelu_pull(grad_hidden)[0].astype(jnp.bfloat16)
    grad_fc1 = jnp.einsum("rd,rf->df", h_second, grad_pre, preferred_element_type=jnp.float32)
    grad_bfc1 = jnp.sum(grad_pre.astype(jnp.float32), axis=0)
    grad_h2 = jnp.einsum("rf,df->rd", grad_pre, full_fc1, preferred_element_type=jnp.float32)
    second_pull = jax.vjp(modulate, middle, pieces[3], pieces[4])[1]
    grad_mid_norm, grad_shift_two, grad_scale_two = second_pull(grad_h2)
    grad_mid = grad_res + grad_mid_norm
    grad_branch = (pieces[2] * grad_mid).astype(jnp.bfloat16)
    grad_gate_one = jnp.sum(grad_mid * branch, axis=0)
    grad_proj = jnp.einsum("rd,re->de", attended, grad_branch, preferred_element_type=jnp.float32)
    grad_bproj = jnp.sum(grad_branch.astype(jnp.float32), axis=0)
    grad_att = jnp.einsum(
        "re,de->rd", grad_branch, full_proj, preferred_element_type=jnp.float32
    ).astype(jnp.bfloat16)
    grad_att = grad_att.reshape(images // 2, 2, length, heads, HEAD_DIM)
    grad_qkv = lax.map(
        attend_back,
        (
            split_rows[:, :, :, 0],
            split_rows[:, :, :, 1],
            split_rows[:, :, :, 2],
            log_total,
            grad_att,
        ),
    )
    grad_qkv = grad_qkv.reshape(images * length, 3 * width).astype(jnp.bfloat16)
    grad_wqkv = jnp.einsum("rd,re->de", h_first, grad_qkv, preferred_element_type=jnp.float32)
    qkv_sums = jnp.sum(grad_qkv.astype(jnp.float32), axis=0)
    grad_bqv = jnp.concatenate([qkv_sums[:width], qkv_sums[2 * width :]])
    grad_h1 = jnp.einsum("re,de->rd", grad_qkv, full_qkv, preferred_element_type=jnp.float32)
    first_pull = jax.vjp(modulate, flat_rows, pieces[0], pieces[1])[1]
    grad_rows_norm, grad_shift_one, grad_scale_one = first_pull(grad_h1)
    grad_rows = grad_mid + grad_rows_norm
    grad_mod = jnp.concatenate(
        [
            grad_shift_one,
            grad_scale_one,
            grad_gate_one,
            grad_shift_two,
            grad_scale_two,
            grad_gate_two,
        ]
    )
    shards = (
        lax.psum_scatter(grad_wqkv, "fsdp", scatter_dimension=0, tiled=True),
        lax.psum_scatter(grad_proj, "fsdp", scatter_dimension=0, tiled=True),
        lax.psum_scatter(grad_fc1, "fsdp", scatter_dimension=0, tiled=True),
        lax.psum_scatter(grad_fc2, "fsdp", scatter_dimension=0, tiled=True),
        lax.psum_scatter(grad_bqv, "fsdp", scatter_dimension=0, tiled=True),
        lax.psum_scatter(grad_bproj, "fsdp", scatter_dimension=0, tiled=True),
        lax.psum_scatter(grad_bfc1, "fsdp", scatter_dimension=0, tiled=True),
        lax.psum_scatter(grad_bfc2, "fsdp", scatter_dimension=0, tiled=True),
        lax.psum_scatter(grad_mod, "fsdp", scatter_dimension=0, tiled=True),
    )
    mod_mine = shards[8]
    grad_wada = scaled.astype(jnp.float32)[:, None] * mod_mine[None, :]
    grad_scaled = jnp.dot(w_ada.astype(jnp.float32), mod_mine, precision=lax.Precision.HIGHEST)
    grad_scaled = lax.psum(grad_scaled, "fsdp")
    silu_pull = jax.vjp(jax.nn.silu, cond[0])[1]
    grad_cond = silu_pull(grad_scaled)[0][None, :]
    totals = lax.psum(
        (
            shards[0],
            shards[1],
            shards[2],
            shards[3],
            shards[4],
            shards[5],
            shards[6],
            shards[7],
            grad_wada,
            mod_mine,
        ),
        "bin",
    )
    return (
        block_out,
        grad_rows.reshape(latents.shape),
        grad_cond,
        totals[8],
        totals[9],
        totals[0],
        totals[4],
        totals[1],
        totals[5],
        totals[2],
        totals[6],
        totals[3],
        totals[7],
    )


def solution(mesh):
    return jax.shard_map(
        on_device,
        mesh=mesh,
        in_specs=(
            P("bin", "fsdp", None, None),
            P("bin", None),
            P("bin", "fsdp"),
            P(None, "fsdp"),
            P("fsdp"),
            P("fsdp", None),
            P("fsdp"),
            P("fsdp", None),
            P("fsdp"),
            P("fsdp", None),
            P("fsdp"),
            P("fsdp", None),
            P("fsdp"),
            P("bin", "fsdp", None, None),
        ),
        out_specs=(
            P("bin", "fsdp", None, None),
            P("bin", "fsdp", None, None),
            P("bin", None),
            P(None, "fsdp"),
            P("fsdp"),
            P("fsdp", None),
            P("fsdp"),
            P("fsdp", None),
            P("fsdp"),
            P("fsdp", None),
            P("fsdp"),
            P("fsdp", None),
            P("fsdp"),
        ),
        check_vma=False,
    )
```

profile of v0, /device:TPU:0, one launch (start us, length us, event | category | flops | bytes accessed | tf_op | source)
XLA Modules:
  0.0 1843.6 jit_solution(338678586922015093)
XLA Ops:
  16.1 40.7 %all-reduce.13 = (bf16[2304]{0:T(1024)(128)(2,1)S(1)}, bf16[1152]{0:T(1024)(128)(2,1)S(1)}, bf16[1152]{0:T(1024)(128)(2,1)}, bf16[4608]{0:T(1024)(128)(2,1)S(1)}) all-reduce(bf16[2304]{0:T(1024)(128)(2,1)S(1)} %dynamic-update-slice.1, bf16[1152]{0:T(1024)(128)(2,1)S(1)} %dynamic-update-slice.2, ...), channel_id=1, replica_groups=mesh['bin'=4,'fsdp'=8] {'fsdp'}, use_global_device_ids=true, to_apply=%add.1 | all-reduce | flops 9216 | bytes 36864
  58.9 34.5 %all-reduce = f32[6912]{0:T(1024)S(1)} all-reduce(f32[6912]{0:T(1024)S(1)} %add_dynamic-update-slice_fusion), channel_id=1, replica_groups=mesh['bin'=4,'fsdp'=8] {'fsdp'}, use_global_device_ids=true, to_apply=%add | all-reduce | flops 6912 | bytes 55296
  97.7 36.3 %all-gather.5.cloned.1.call-done = bf16[1152,3456]{1,0:T(8,128)(2,1)} async-done(((bf16[144,3456]{1,0:T(8,128)(2,1)}), bf16[1152,3456]{1,0:T(8,128)(2,1)}) %all-gather.5.cloned.1.call-update) | async-done | bytes 7962640 | tf_op jit(solution)/shard_map/all_gather | solution.py:140
  134.0 10.3 add_convert_fusion
  144.3 13.6 reshape.274
  182.6 14.0 fusion.32
  206.9 135.9 %all-gather.9.cloned.1.call-done = bf16[1152,4608]{1,0:T(8,128)(2,1)} async-done(((bf16[144,4608]{1,0:T(8,128)(2,1)}), bf16[1152,4608]{1,0:T(8,128)(2,1)}) %all-gather.9.cloned.1.call-update) | async-done | bytes 10616848 | tf_op jit(solution)/shard_map/all_gather | solution.py:142
  342.8 12.2 fusion.51
  355.0 140.5 %all-gather.11.cloned.1.call-done = bf16[4608,1152]{1,0:T(8,128)(2,1)} async-done(((bf16[576,1152]{1,0:T(8,128)(2,1)}), bf16[4608,1152]{1,0:T(8,128)(2,1)}) %all-gather.11.cloned.1.call-update) | async-done | bytes 10616848 | tf_op jit(solution)/shard_map/all_gather | solution.py:143
  495.5 18.9 %convert_reduce_fusion = (f32[4608]{0:T(1024)S(1)}, bf16[512,4608]{1,0:T(8,128)(2,1)}) fusion(f32[512,4608]{1,0:T(8,128)} %fusion.51, f32[4608]{0:T(1024)S(1)} %convert_element_type.166, bf16[512,1152]{1,0:T(8,128)(2,1)} %multiply_convert_fusion.4, bf16[4608,1152]{1,0:T(8,128)(2,1)} %all-gather.11.cloned.1.call-done), kind=kOutput, calls=%fused_computation.10 | convolution fusion | flops 5499514368 | bytes 25989120 | tf_op jit(solution)/shard_map/rd,fd->rf/dot_general | solution.py:185
  514.3 11.6 multiply_reduce_fusion.3
  549.7 6.6 multiply_reduce_fusion
  572.9 7.9 fusion.62
  580.9 13.0 fusion.50
  594.0 14.8 fusion.52
  610.2 9.9 fusion.27
  622.2 15.5 multiply_reduce_fusion.2
  637.8 35.9 %all-reduce.5 = f32[6912]{0:T(1024)S(1)} all-reduce(f32[6912]{0:T(1024)S(1)} %constant_dynamic-update-slice_fusion), channel_id=2, replica_groups=mesh['bin'=4,'fsdp'=8] {'fsdp'}, use_global_device_ids=true, to_apply=%region_17.18.clone | all-reduce | flops 6912 | bytes 55296
  676.0 232.5 %reduce-scatter.5.cloned.1.call-done = f32[144,3456]{1,0:T(8,128)} async-done(((f32[1152,3456]{1,0:T(8,128)}), f32[144,3456]{1,0:T(8,128)}) %reduce-scatter.5.cloned.1.call-update) | async-done | bytes 1990672 | tf_op jit(solution)/shard_map/reduce_scatter | solution.py:231
  908.6 350.7 %reduce-scatter.9.cloned.1.call-done = f32[144,4608]{1,0:T(8,128)} async-done(((f32[1152,4608]{1,0:T(8,128)}), f32[144,4608]{1,0:T(8,128)}) %reduce-scatter.9.cloned.1.call-update) | async-done | bytes 2654224 | tf_op jit(solution)/shard_map/reduce_scatter | solution.py:233
  1259.3 350.3 %reduce-scatter.11.cloned.1.call-done = f32[576,1152]{1,0:T(8,128)} async-done(((f32[4608,1152]{1,0:T(8,128)}), f32[576,1152]{1,0:T(8,128)}) %reduce-scatter.11.cloned.1.call-update) | async-done | bytes 2654224 | tf_op jit(solution)/shard_map/reduce_scatter | solution.py:234
  1613.2 35.7 %all-reduce.10 = (f32[1152]{0:T(1024)S(1)}, f32[2304]{0:T(1024)S(1)}, f32[1152]{0:T(1024)S(1)}, f32[4608]{0:T(1024)S(1)}, f32[1152]{0:T(1024)S(1)}) all-reduce(f32[1152]{0:T(1024)S(1)} %convolution_reduce_fusion, f32[2304]{0:T(1024)S(1)} %pad_maximum_fusion, ...), channel_id=1, replica_groups=mesh['bin'=4,'fsdp'=8] {'fsdp'}, use_global_device_ids=true, to_apply=%region_18.19 | all-reduce | flops 10368 | bytes 82944 | tf_op jit(solution)/shard_map/psum | solution.py:244
  1649.9 12.5 all-reduce.11
  1662.4 162.9 %all-reduce.16.cloned.1.call-done = (f32[1152,864]{0,1:T(8,128)}, f32[144,3456]{1,0:T(8,128)}, f32[144,1152]{1,0:T(8,128)}, f32[144,4608]{1,0:T(8,128)}, f32[576,1152]{1,0:T(8,128)}) async-done(((f32[1152,864]{0,1:T(8,128)}, f32[144,3456]{1,0:T(8,128)}, f32[144,1152]{1,0:T(8,128)}, f32[144,4608]{1,0:T(8,128)}, f32[576,1152]{1,0:T(8,128)}), (f32[1152,864]{0,1:T(8,128)}, f32[144,3456]{1,0:T(8,128)}, ...) | async-done | bytes 11943952 | tf_op jit(solution)/shard_map/psum | solution.py:247
  (210 shorter events, 106.1 us)
Async XLA Ops:
  7.2 51.0 %copy-start = (bf16[1152,864]{0,1:T(8,128)(2,1)S(1)}, bf16[1152,864]{0,1:T(8,128)(2,1)}, u32[]{:S(2)}) copy-start(bf16[1152,864]{0,1:T(8,128)(2,1)} %param.17) | copy-start | bytes 5971972
  7.2 8.7 copy-start.41
  7.3 49.6 %copy-start.2 = (bf16[1,2,256,1152]{3,2,1,0:T(8,128)(2,1)S(1)}, bf16[1,2,256,1152]{3,2,1,0:T(8,128)(2,1)}, u32[]{:S(2)}) copy-start(bf16[1,2,256,1152]{3,2,1,0:T(8,128)(2,1)} %param.14) | copy-start | bytes 3538948
  7.3 126.8 %all-gather.5.cloned.1.call-start = ((), (), s32[]{:S(2)}) async-start(), calls=%async_computation.4 | async-start | bytes 8957952 | tf_op jit(solution)/shard_map/all_gather | solution.py:140
  8.0 191.1 %all-gather.7.cloned.1.call-start = ((), (), s32[]{:S(2)}) async-start(), calls=%async_computation.5 | async-start | bytes 2985984 | tf_op jit(solution)/shard_map/all_gather | solution.py:141
  8.8 334.0 %all-gather.9.cloned.1.call-start = ((), (), s32[]{:S(2)}) async-start(), calls=%async_computation.6 | async-start | bytes 11943936 | tf_op jit(solution)/shard_map/all_gather | solution.py:142
  9.5 486.0 %all-gather.11.cloned.1.call-start = ((), (), s32[]{:S(2)}) async-start(), calls=%async_computation.7 | async-start | bytes 11943936 | tf_op jit(solution)/shard_map/all_gather | solution.py:143
  10.1 48.7 %copy-start.42 = (bf16[864]{0:T(1024)(128)(2,1)S(1)}, bf16[864]{0:T(1024)(128)(2,1)}, u32[]{:S(2)}) copy-start(bf16[864]{0:T(1024)(128)(2,1)} %param.18) | copy-start | bytes 5188
  10.1 666.0 %reduce-scatter.7.cloned.1.call-start = ((), (), s32[]{:S(2)}) async-start(), calls=%async_computation.9 | async-start | bytes 5971968 | tf_op jit(solution)/shard_map/reduce_scatter | solution.py:232
  11.3 82.2 %copy-start.27 = (f32[1152]{0:T(1024)}, f32[1152]{0:T(1024)S(1)}, u32[]{:S(2)}) copy-start(f32[1152]{0:T(1024)S(1)} %reduce.4) | copy-start | bytes 13828
  58.1 39.6 %copy-start.30 = (f32[512]{0:T(512)}, f32[512]{0:T(512)S(1)}, u32[]{:S(2)}) copy-start(f32[512]{0:T(512)S(1)} %rsqrt.27) | copy-start | bytes 6148
  58.1 39.6 %copy-start.32 = (f32[1,2,2,128]{3,1,2,0:T(2,128)}, f32[1,2,2,128]{3,1,2,0:T(2,128)S(1)}, u32[]{:S(2)}) copy-start(f32[1,2,2,128]{3,1,2,0:T(2,128)S(1)} %copy.73) | copy-start | bytes 6148
  495.5 18.9 %copy-start.4 = (f32[512,1152]{1,0:T(8,128)S(1)}, f32[512,1152]{1,0:T(8,128)}, u32[]{:S(2)}) copy-start(f32[512,1152]{1,0:T(8,128)} %copy-done.3) | copy-start | bytes 7077892
  533.2 375.4 %reduce-scatter.5.cloned.1.call-start = ((), (), s32[]{:S(2)}) async-start(), calls=%async_computation.8 | async-start | bytes 17915904 | tf_op jit(solution)/shard_map/reduce_scatter | solution.py:231
  549.7 13.8 slice-start
  580.9 678.4 %reduce-scatter.9.cloned.1.call-start = ((), (), s32[]{:S(2)}) async-start(), calls=%async_computation.10 | async-start | bytes 23887872 | tf_op jit(solution)/shard_map/reduce_scatter | solution.py:233
  594.0 1015.7 %reduce-scatter.11.cloned.1.call-start = ((), (), s32[]{:S(2)}) async-start(), calls=%async_computation.11 | async-start | bytes 23887872 | tf_op jit(solution)/shard_map/reduce_scatter | solution.py:234
  608.9 1216.4 %all-reduce.16.cloned.1.call-start = ((), (), s32[]{:S(2)}) async-start(), calls=%async_computation.12 | async-start | bytes 23887872 | tf_op jit(solution)/shard_map/psum | solution.py:247
  610.2 10.0 copy-start.35
  610.2 10.0 copy-start.31
  610.2 11.2 copy-start.13
  610.2 11.2 copy-start.19
  622.2 51.6 %copy-start.29 = (f32[1152]{0:T(1024)S(1)}, f32[1152]{0:T(1024)}, u32[]{:S(2)}) copy-start(f32[1152]{0:T(1024)} %get-tuple-element.94) | copy-start | bytes 13828
  1609.7 39.3 %copy-start.28 = (f32[1152]{0:T(1024)S(1)}, f32[1152]{0:T(1024)}, u32[]{:S(2)}) copy-start(f32[1152]{0:T(1024)} %copy-done.27) | copy-start | bytes 13828
  (33 other events, 96.3 us)
Sparse Core Ops, SparseCore 0:
  10.3 123.7 all-gather.4
  136.2 53.2 all-gather.6
  191.7 151.0 all-gather.8
  344.8 150.6 all-gather.10
  533.3 102.3 reduce-scatter.6
  639.9 268.5 reduce-scatter.4
  912.9 346.3 reduce-scatter.8
  1263.2 346.4 reduce-scatter.10
  1613.5 211.7 all-reduce.15
where the time goes:
time: 1850 us; the launch traced here: 1840 us
  waiting for transfers between devices  1410 us (76%)
  blocking collectives  159 us (9%)
  matrix products  158 us (9%)
  local copies, waits for them, and re-layouts  72.8 us (4%)
  between operations  20.8 us (1%)
  other arithmetic  20.4 us (1%)
    reduce_scatter x1, waiting for transfers between devices, on_device(): lax.psum_scatter(grad_fc1, 'fsdp', scatter_dimension=0, tiled=True)  351 us
    reduce_scatter x1, waiting for transfers between devices, on_device(): lax.psum_scatter(grad_fc2, 'fsdp', scatter_dimension=0, tiled=True)  350 us
    reduce_scatter x1, waiting for transfers between devices, on_device(): lax.psum_scatter(grad_wqkv, 'fsdp', scatter_dimension=0, tiled=True)  233 us
    psum x1, waiting for transfers between devices, on_device(): lax.psum((shards[0], shards[1], shards[2], shards[3], shards[4], shards[5...  163 us
    all_gather x1, waiting for transfers between devices, on_device(): lax.all_gather(w_fc2, 'fsdp', axis=0, tiled=True)  140 us
    all_gather x1, waiting for transfers between devices, on_device(): lax.all_gather(w_fc1, 'fsdp', axis=0, tiled=True)  136 us
    unnamed x3, blocking collectives  111 us
    unnamed x128, local copies, waits for them, and re-layouts  37.7 us
  transfers between devices with their start and end apart: 9, of which 7 were waited for; matrix products, arithmetic and copies ran while one was open for 11% of the time, Pallas kernels for 0%

commit v1 on v0

--- a/solution.py
+++ b/solution.py
@@ -4,6 +4,25 @@
 from jax.sharding import PartitionSpec as P
 
 HEAD_DIM = 72
+
+
+def produce_positions(s0, row_axis):
+    n_dev_all = lax.psum(1, axis_name=row_axis)
+    vals = []
+    for hop_no in range(n_dev_all):
+        vals.append((hop_no, (hop_no + 1) % n_dev_all))
+    inbox = []
+    for hop_no in range(n_dev_all):
+        inbox.append((hop_no, (hop_no - 1) % n_dev_all))
+    t1, z2 = ([s0], [s0])
+    for _ in range(n_dev_all // 2):
+        t1.append(lax.ppermute(t1[-1], axis_name=row_axis, perm=vals))
+    for _ in range((n_dev_all - 1) // 2):
+        big = lax.ppermute(z2[-1], axis_name=row_axis, perm=inbox)
+        z2.append(big)
+    b_next = jnp.concatenate([*t1[::-1], *z2[1:]], axis=0)
+    built = jnp.roll(b_next, (lax.axis_index(row_axis) - n_dev_all // 2) * s0.shape[0], axis=0)
+    return built
 
 
 def layer_norm(field):
@@ -140,7 +159,7 @@
         lax.all_gather(w_qkv, "fsdp", axis=0, tiled=True),
         lax.all_gather(w_proj, "fsdp", axis=0, tiled=True),
         lax.all_gather(w_fc1, "fsdp", axis=0, tiled=True),
-        lax.all_gather(w_fc2, "fsdp", axis=0, tiled=True),
+        produce_positions(w_fc2, "fsdp"),
         lax.all_gather(b_qv, "fsdp", axis=0, tiled=True),
         lax.all_gather(b_proj, "fsdp", axis=0, tiled=True),
         lax.all_gather(b_fc1, "fsdp", axis=0, tiled=True),

time: 1850 us -> 1960 us (1.059)
  waiting for transfers between devices: 1410 us -> 1480 us
  local copies, waits for them, and re-layouts: 72.8 us -> 109 us
    ppermute x0 -> x7, waiting for transfers between devices: none -> 251 us  [the longest x4 247 us: produce_positions(): t1.append(lax.ppermute(t1[-1], axis_name=row_axis, perm=vals))]
    reduce_scatter x1, waiting for transfers between devices: 233 us -> 68.3 us  [on_device(): lax.psum_scatter(grad_wqkv, 'fsdp', scatter_dimension=0, tiled=True)]
    psum x1, waiting for transfers between devices: 163 us -> 128 us  [on_device(): lax.psum((shards[0], shards[1], shards[2], shards[3], shards[4], shards[5...]
    unnamed x128 -> x165, local copies, waits for them, and re-layouts: 37.7 us -> 70.9 us
  transfers between devices with their start and end apart: 9 -> 16, of which waited for: 7 -> 13; matrix products, arithmetic and copies ran while one was open for 11% -> 12% of each run, Pallas kernels for 0% -> 0%
where the time goes in v1:
time: 1960 us; the launch traced here: 1950 us
  waiting for transfers between devices  1480 us (76%)
  blocking collectives  158 us (8%)
  matrix products  151 us (8%)
  local copies, waits for them, and re-layouts  109 us (6%)
  other arithmetic  25.5 us (1%)
  between operations  20.7 us (1%)
    reduce_scatter x1, waiting for transfers between devices, on_device(): lax.psum_scatter(grad_fc1, 'fsdp', scatter_dimension=0, tiled=True)  351 us
    reduce_scatter x1, waiting for transfers between devices, on_device(): lax.psum_scatter(grad_fc2, 'fsdp', scatter_dimension=0, tiled=True)  350 us
    ppermute x4, waiting for transfers between devices, produce_positions(): t1.append(lax.ppermute(t1[-1], axis_name=row_axis, perm=vals))  247 us
    all_gather x1, waiting for transfers between devices, on_device(): lax.all_gather(w_fc1, 'fsdp', axis=0, tiled=True)  146 us
    all_gather x1, waiting for transfers between devices, on_device(): lax.all_gather(w_fc2, 'fsdp', axis=0, tiled=True)  138 us
    psum x1, waiting for transfers between devices, on_device(): lax.psum((shards[0], shards[1], shards[2], shards[3], shards[4], shards[5...  128 us
    unnamed x3, blocking collectives  111 us
    unnamed x165, local copies, waits for them, and re-layouts  70.9 us
  transfers between devices with their start and end apart: 16, of which 13 were waited for; matrix products, arithmetic and copies ran while one was open for 12% of the time, Pallas kernels for 0%

profile of v1, /device:TPU:0, one launch (start us, length us, event | category | flops | bytes accessed | tf_op | source)
XLA Modules:
  0.0 1952.2 jit_solution(4138245054828328226)
XLA Ops:
  15.8 40.8 %all-reduce.13 = (bf16[2304]{0:T(1024)(128)(2,1)S(1)}, bf16[1152]{0:T(1024)(128)(2,1)S(1)}, bf16[4608]{0:T(1024)(128)(2,1)S(1)}, bf16[1152]{0:T(1024)(128)(2,1)}) all-reduce(bf16[2304]{0:T(1024)(128)(2,1)S(1)} %dynamic-update-slice.1, bf16[1152]{0:T(1024)(128)(2,1)S(1)} %dynamic-update-slice.2, ...), channel_id=1, replica_groups=mesh['bin'=4,'fsdp'=8] {'fsdp'}, use_global_device_ids=true, to_apply=%add.1 | all-reduce | flops 9216 | bytes 36864
  58.1 34.3 %all-reduce = f32[6912]{0:T(1024)S(1)} all-reduce(f32[6912]{0:T(1024)S(1)} %add_dynamic-update-slice_fusion), channel_id=1, replica_groups=mesh['bin'=4,'fsdp'=8] {'fsdp'}, use_global_device_ids=true, to_apply=%add | all-reduce | flops 6912 | bytes 55296
  95.6 38.4 %all-gather.5.cloned.1.call-done = bf16[1152,3456]{1,0:T(8,128)(2,1)} async-done(((bf16[144,3456]{1,0:T(8,128)(2,1)}), bf16[1152,3456]{1,0:T(8,128)(2,1)}) %all-gather.5.cloned.1.call-update) | async-done | bytes 7962640 | tf_op jit(solution)/shard_map/all_gather | solution.py:159
  134.0 10.3 add_convert_fusion
  144.3 13.6 reshape.274
  196.9 145.9 %all-gather.9.cloned.1.call-done = bf16[1152,4608]{1,0:T(8,128)(2,1)} async-done(((bf16[144,4608]{1,0:T(8,128)(2,1)}), bf16[1152,4608]{1,0:T(8,128)(2,1)}) %all-gather.9.cloned.1.call-update) | async-done | bytes 10616848 | tf_op jit(solution)/shard_map/all_gather | solution.py:161
  342.8 14.4 multiply_convert_fusion
  357.2 138.3 %all-gather.11.cloned.1.call-done = bf16[4608,1152]{1,0:T(8,128)(2,1)} async-done(((bf16[576,1152]{1,0:T(8,128)(2,1)}), bf16[4608,1152]{1,0:T(8,128)(2,1)}) %all-gather.11.cloned.1.call-update) | async-done | bytes 10616848 | tf_op jit(solution)/shard_map/all_gather | solution.py:177
  495.5 18.2 convert_reduce_fusion
  513.7 12.3 multiply_reduce_fusion.2
  582.4 13.0 fusion.72
  595.4 13.3 fusion.60
  609.4 54.5 %collective-permute-done = bf16[576,1152]{1,0:T(8,128)(2,1)S(1)} collective-permute-done((bf16[576,1152]{1,0:T(8,128)(2,1)}, bf16[576,1152]{1,0:T(8,128)(2,1)S(1)}, u32[]{:S(2)}, u32[]{:S(2)}) %collective-permute-start) | collective-permute-done | bytes 1327136 | tf_op jit(solution)/shard_map/ppermute | solution.py:19
  669.7 63.7 %collective-permute-done.1 = bf16[576,1152]{1,0:T(8,128)(2,1)S(1)} collective-permute-done((bf16[576,1152]{1,0:T(8,128)(2,1)S(1)}, bf16[576,1152]{1,0:T(8,128)(2,1)S(1)}, u32[]{:S(2)}, u32[]{:S(2)}) %collective-permute-start.1) | collective-permute-done | bytes 1327136 | tf_op jit(solution)/shard_map/ppermute | solution.py:19
  740.9 68.2 %collective-permute-done.2 = bf16[576,1152]{1,0:T(8,128)(2,1)} collective-permute-done((bf16[576,1152]{1,0:T(8,128)(2,1)S(1)}, bf16[576,1152]{1,0:T(8,128)(2,1)}, u32[]{:S(2)}, u32[]{:S(2)}) %collective-permute-start.2) | collective-permute-done | bytes 1327136 | tf_op jit(solution)/shard_map/ppermute | solution.py:19
  818.2 60.9 %collective-permute-done.3 = bf16[576,1152]{1,0:T(8,128)(2,1)} collective-permute-done((bf16[576,1152]{1,0:T(8,128)(2,1)}, bf16[576,1152]{1,0:T(8,128)(2,1)}, u32[]{:S(2)}, u32[]{:S(2)}) %collective-permute-start.3) | collective-permute-done | bytes 1327136 | tf_op jit(solution)/shard_map/ppermute | solution.py:19
  911.0 35.5 %all-reduce.5 = f32[6912]{0:T(1024)S(1)} all-reduce(f32[6912]{0:T(1024)S(1)} %constant_dynamic-update-slice_fusion.17), channel_id=2, replica_groups=mesh['bin'=4,'fsdp'=8] {'fsdp'}, use_global_device_ids=true, to_apply=%region_17.18.clone | all-reduce | flops 6912 | bytes 55296
  949.0 68.3 %reduce-scatter.5.cloned.1.call-done = f32[144,3456]{1,0:T(8,128)} async-done(((f32[1152,3456]{1,0:T(8,128)}), f32[144,3456]{1,0:T(8,128)}) %reduce-scatter.5.cloned.1.call-update) | async-done | bytes 1990672 | tf_op jit(solution)/shard_map/reduce_scatter | solution.py:250
  1017.3 350.7 %reduce-scatter.9.cloned.1.call-done = f32[144,4608]{1,0:T(8,128)} async-done(((f32[1152,4608]{1,0:T(8,128)}), f32[144,4608]{1,0:T(8,128)}) %reduce-scatter.9.cloned.1.call-update) | async-done | bytes 2654224 | tf_op jit(solution)/shard_map/reduce_scatter | solution.py:252
  1368.0 350.3 %reduce-scatter.11.cloned.1.call-done = f32[576,1152]{1,0:T(8,128)} async-done(((f32[4608,1152]{1,0:T(8,128)}), f32[576,1152]{1,0:T(8,128)}) %reduce-scatter.11.cloned.1.call-update) | async-done | bytes 2654224 | tf_op jit(solution)/shard_map/reduce_scatter | solution.py:253
  1741.1 35.3 %all-reduce.10 = (f32[1152]{0:T(1024)S(1)}, f32[2304]{0:T(1024)S(1)}, f32[1152]{0:T(1024)S(1)}, f32[4608]{0:T(1024)S(1)}, f32[1152]{0:T(1024)S(1)}) all-reduce(f32[1152]{0:T(1024)S(1)} %convolution_reduce_fusion, f32[2304]{0:T(1024)S(1)} %pad_maximum_fusion, ...), channel_id=1, replica_groups=mesh['bin'=4,'fsdp'=8] {'fsdp'}, use_global_device_ids=true, to_apply=%region_18.19 | all-reduce | flops 10368 | bytes 82944 | tf_op jit(solution)/shard_map/psum | solution.py:263
  1777.4 11.7 all-reduce.11
  1793.6 12.4 fusion.28
  1806.0 127.9 %all-reduce.16.cloned.1.call-done = (f32[1152,864]{0,1:T(8,128)}, f32[144,3456]{1,0:T(8,128)}, f32[144,1152]{1,0:T(8,128)}, f32[144,4608]{1,0:T(8,128)}, f32[576,1152]{1,0:T(8,128)}) async-done(((f32[1152,864]{0,1:T(8,128)}, f32[144,3456]{1,0:T(8,128)}, f32[144,1152]{1,0:T(8,128)}, f32[144,4608]{1,0:T(8,128)}, f32[576,1152]{1,0:T(8,128)}), (f32[1152,864]{0,1:T(8,128)}, f32[144,3456]{1,0:T(8,128)}, ...) | async-done | bytes 11943952 | tf_op jit(solution)/shard_map/psum | solution.py:266
  (265 shorter events, 199.6 us)
Async XLA Ops:
  7.2 50.2 %copy-start = (bf16[1152,864]{0,1:T(8,128)(2,1)S(1)}, bf16[1152,864]{0,1:T(8,128)(2,1)}, u32[]{:S(2)}) copy-start(bf16[1152,864]{0,1:T(8,128)(2,1)} %param.17) | copy-start | bytes 5971972
  7.2 126.7 %all-gather.5.cloned.1.call-start = ((), (), s32[]{:S(2)}) async-start(), calls=%async_computation.4 | async-start | bytes 8957952 | tf_op jit(solution)/shard_map/all_gather | solution.py:159
  8.0 181.5 %all-gather.7.cloned.1.call-start = ((), (), s32[]{:S(2)}) async-start(), calls=%async_computation.5 | async-start | bytes 2985984 | tf_op jit(solution)/shard_map/all_gather | solution.py:160
  8.8 334.0 %all-gather.9.cloned.1.call-start = ((), (), s32[]{:S(2)}) async-start(), calls=%async_computation.6 | async-start | bytes 11943936 | tf_op jit(solution)/shard_map/all_gather | solution.py:161
  9.5 486.0 %all-gather.11.cloned.1.call-start = ((), (), s32[]{:S(2)}) async-start(), calls=%async_computation.7 | async-start | bytes 11943936 | tf_op jit(solution)/shard_map/all_gather | solution.py:177
  10.1 47.9 %copy-start.49 = (bf16[864]{0:T(1024)(128)(2,1)S(1)}, bf16[864]{0:T(1024)(128)(2,1)}, u32[]{:S(2)}) copy-start(bf16[864]{0:T(1024)(128)(2,1)} %param.18) | copy-start | bytes 5188
  10.1 938.9 %reduce-scatter.7.cloned.1.call-start = ((), (), s32[]{:S(2)}) async-start(), calls=%async_computation.9 | async-start | bytes 5971968 | tf_op jit(solution)/shard_map/reduce_scatter | solution.py:251
  13.4 79.1 %copy-start.34 = (f32[1152]{0:T(1024)}, f32[1152]{0:T(1024)S(1)}, u32[]{:S(2)}) copy-start(f32[1152]{0:T(1024)S(1)} %reduce.4) | copy-start | bytes 13828
  14.7 79.2 %copy-start.36 = (f32[512]{0:T(512)}, f32[512]{0:T(512)S(1)}, u32[]{:S(2)}) copy-start(f32[512]{0:T(512)S(1)} %rsqrt.27) | copy-start | bytes 6148
  14.8 79.2 %copy-start.38 = (f32[1,2,2,128]{3,1,2,0:T(2,128)}, f32[1,2,2,128]{3,1,2,0:T(2,128)S(1)}, u32[]{:S(2)}) copy-start(f32[1,2,2,128]{3,1,2,0:T(2,128)S(1)} %copy.73) | copy-start | bytes 6148
  534.7 482.6 %reduce-scatter.5.cloned.1.call-start = ((), (), s32[]{:S(2)}) async-start(), calls=%async_computation.8 | async-start | bytes 17915904 | tf_op jit(solution)/shard_map/reduce_scatter | solution.py:250
  582.3 785.7 %reduce-scatter.9.cloned.1.call-start = ((), (), s32[]{:S(2)}) async-start(), calls=%async_computation.10 | async-start | bytes 23887872 | tf_op jit(solution)/shard_map/reduce_scatter | solution.py:252
  595.4 1122.9 %reduce-scatter.11.cloned.1.call-start = ((), (), s32[]{:S(2)}) async-start(), calls=%async_computation.11 | async-start | bytes 23887872 | tf_op jit(solution)/shard_map/reduce_scatter | solution.py:253
  608.7 202.9 %copy-start.44 = (bf16[1152]{0:T(1024)(128)(2,1)S(1)}, bf16[1152]{0:T(1024)(128)(2,1)}, u32[]{:S(2)}) copy-start(bf16[1152]{0:T(1024)(128)(2,1)} %get-tuple-element.91) | copy-start | bytes 6916
  608.7 205.5 %copy-start.46 = (f32[2]{0:T(128)S(1)}, f32[2]{0:T(128)}, u32[]{:S(2)}) copy-start(f32[2]{0:T(128)} %copy-done.45) | copy-start | bytes 28
  608.8 1325.1 %all-reduce.16.cloned.1.call-start = ((), (), s32[]{:S(2)}) async-start(), calls=%async_computation.12 | async-start | bytes 23887872 | tf_op jit(solution)/shard_map/psum | solution.py:266
  608.8 55.1 %collective-permute-start = (bf16[576,1152]{1,0:T(8,128)(2,1)}, bf16[576,1152]{1,0:T(8,128)(2,1)S(1)}, u32[]{:S(2)}, u32[]{:S(2)}) collective-permute-start(bf16[576,1152]{1,0:T(8,128)(2,1)} %param.25), channel_id=1, source_target_pairs={{0,1},{1,2},{2,3},{3,4},{4,5},{5,6},{6,7},{7,0},{8,9},{9,10},{10,1... | collective-permute-start | bytes 3981320 | tf_op jit(solution)/shard_map/ppermute | solution.py:19
  665.0 68.5 %collective-permute-start.1 = (bf16[576,1152]{1,0:T(8,128)(2,1)S(1)}, bf16[576,1152]{1,0:T(8,128)(2,1)S(1)}, u32[]{:S(2)}, u32[]{:S(2)}) collective-permute-start(bf16[576,1152]{1,0:T(8,128)(2,1)S(1)} %collective-permute-done), channel_id=1, source_target_pairs={{0,1},{1,2},{2,3},{3,4},{4,5},{5,6},{6,7},{7,0},{8,9},{9,10},{10,1... | collective-permute-start | bytes 3981320 | tf_op jit(solution)/shard_map/ppermute | solution.py:19
  665.0 75.9 %collective-permute-start.4 = (bf16[576,1152]{1,0:T(8,128)(2,1)}, bf16[576,1152]{1,0:T(8,128)(2,1)}, u32[]{:S(2)}, u32[]{:S(2)}) collective-permute-start(bf16[576,1152]{1,0:T(8,128)(2,1)} %param.25), channel_id=1, source_target_pairs={{0,7},{1,0},{2,1},{3,2},{4,3},{5,4},{6,5},{7,6},{8,15},{9,8},{10,9... | collective-permute-start | bytes 3981320 | tf_op jit(solution)/shard_map/ppermute | solution.py:21
  734.5 74.6 %collective-permute-start.2 = (bf16[576,1152]{1,0:T(8,128)(2,1)S(1)}, bf16[576,1152]{1,0:T(8,128)(2,1)}, u32[]{:S(2)}, u32[]{:S(2)}) collective-permute-start(bf16[576,1152]{1,0:T(8,128)(2,1)S(1)} %collective-permute-done.1), channel_id=1, source_target_pairs={{0,1},{1,2},{2,3},{3,4},{4,5},{5,6},{6,7},{7,0},{8,9},{9,10},{10,1... | collective-permute-start | bytes 3981320 | tf_op jit(solution)/shard_map/ppermute | solution.py:19
  740.9 75.1 %collective-permute-start.5 = (bf16[576,1152]{1,0:T(8,128)(2,1)}, bf16[576,1152]{1,0:T(8,128)(2,1)}, u32[]{:S(2)}, u32[]{:S(2)}) collective-permute-start(bf16[576,1152]{1,0:T(8,128)(2,1)} %collective-permute-done.4), channel_id=1, source_target_pairs={{0,7},{1,0},{2,1},{3,2},{4,3},{5,4},{6,5},{7,6},{8,15},{9,8},{10,9... | collective-permute-start | bytes 3981320 | tf_op jit(solution)/shard_map/ppermute | solution.py:21
  809.1 70.0 %collective-permute-start.3 = (bf16[576,1152]{1,0:T(8,128)(2,1)}, bf16[576,1152]{1,0:T(8,128)(2,1)}, u32[]{:S(2)}, u32[]{:S(2)}) collective-permute-start(bf16[576,1152]{1,0:T(8,128)(2,1)} %collective-permute-done.2), channel_id=1, source_target_pairs={{0,1},{1,2},{2,3},{3,4},{4,5},{5,6},{6,7},{7,0},{8,9},{9,10},{10,1... | collective-permute-start | bytes 3981320 | tf_op jit(solution)/shard_map/ppermute | solution.py:19
  816.0 68.2 %copy-start.20 = (bf16[576,1152]{1,0:T(8,128)(2,1)S(1)}, bf16[576,1152]{1,0:T(8,128)(2,1)}, u32[]{:S(2)}) copy-start(bf16[576,1152]{1,0:T(8,128)(2,1)} %copy-done.19) | copy-start | bytes 3981316
  816.0 904.8 %collective-permute-start.6 = (bf16[576,1152]{1,0:T(8,128)(2,1)}, bf16[576,1152]{1,0:T(8,128)(2,1)}, u32[]{:S(2)}, u32[]{:S(2)}) collective-permute-start(bf16[576,1152]{1,0:T(8,128)(2,1)} %collective-permute-done.5), channel_id=1, source_target_pairs={{0,7},{1,0},{2,1},{3,2},{4,3},{5,4},{6,5},{7,6},{8,15},{9,8},{10,9... | collective-permute-start | bytes 3981320 | tf_op jit(solution)/shard_map/ppermute | solution.py:21
  (51 other events, 360.1 us)
Sparse Core Ops, SparseCore 0:
  10.2 123.6 all-gather.4
  136.1 53.3 all-gather.6
  191.7 151.0 all-gather.8
  344.8 150.6 all-gather.10
  534.8 107.5 reduce-scatter.6
  646.6 370.5 reduce-scatter.4
  1021.6 346.2 reduce-scatter.8
  1371.9 346.3 reduce-scatter.10
  1722.1 211.7 all-reduce.15
